TPU v7x, 32 devices: a whole 2x2x4 slice. The times are simulated.
32 devices in a mesh: stream: 8 (over y, x, core), tp: 4 (over z).
Axes of the slice: x: 2, y: 2, z: 4, core: 2. Of those that a mesh axis runs over, the one named last changes fastest.
Arguments:
- tokens: bfloat16 [12288, 3072], P('stream', 'tp'), may hold values from -6 to 6
- qkv_weight: bfloat16 [3072, 3, 2048], P('stream', None, 'tp'), may hold values from -0.109375 to 0.109375
- gate_weight: bfloat16 [3072, 2048], P('stream', 'tp'), may hold values from -0.109375 to 0.109375
- out_weight: bfloat16 [2048, 3072], P('tp', 'stream'), may hold values from -0.125 to 0.125
- log_decay: float32 [32, 12288], P('tp', 'stream'), may hold values from -1 to 0
- states: float32 [96, 32, 64, 64], P('stream', 'tp'), may hold values from -48 to 48
- dest_slot: int32 [96], P('stream'), may hold values from 0 to 95, as said below
- valid: int32 [96], P('stream'), may hold values from 1 to 128
Outputs:
- mixed: bfloat16 [12288, 3072], P('stream', 'tp')
- new_states: float32 [96, 32, 64, 64], P('stream', 'tp')
Inputs may be any that keep to these rules, and one draw needn't show every extreme that they name: dest_slot is a permutation of the streams; of the 12 streams of one device, at most 2 have new positions on any one device, and that many do for some pair of devices.
All inputs are finite; a program needn't handle non-finite values.
Results may differ from a plain program's by a relative error of at most 0.0058.
Values may be sent and summed in bfloat16 or wider, within the bound.
A program may use at most 128 MiB of HBM per device.

v0:
```python
import jax
import jax.numpy as jnp
from jax import lax
from jax.sharding import PartitionSpec as P

HD = 64
WINDOW_LENGTH = 128


def move_states(states, dest_slot):
    streams = states.shape[0]
    node_count = lax.axis_size("stream")
    capacity = (streams + node_count - 1) // node_count
    target = dest_slot // streams
    places = dest_slot % streams
    order = jnp.arange(streams, dtype=jnp.int32)
    earlier = (target[None, :] == target[:, None]) & (order[None, :] < order[:, None])
    ranking = jnp.sum(earlier.astype(jnp.int32), axis=1)
    position = target * capacity + ranking
    tail_shape = states.shape[1:]
    outgoing = (
        jnp.zeros((node_count * capacity,) + tail_shape, jnp.float32).at[position].set(states)
    )
    outgoing = outgoing.reshape((node_count, capacity) + tail_shape)
    labels = jnp.full((node_count * capacity,), streams, jnp.int32).at[position].set(places)
    labels = labels.reshape(node_count, capacity)
    incoming, incoming_labels = (
        lax.all_to_all(outgoing, "stream", split_axis=0, concat_axis=0, tiled=True),
        lax.all_to_all(labels, "stream", split_axis=0, concat_axis=0, tiled=True),
    )
    flat_states = incoming.reshape((node_count * capacity,) + tail_shape)
    flat_labels = incoming_labels.reshape(node_count * capacity)
    placed = jnp.zeros((streams + 1,) + tail_shape, jnp.float32).at[flat_labels].set(flat_states)
    return placed[:streams]


def body(tokens, qkv_weight, gate_weight, out_weight, log_decay, states, dest_slot, valid):
    streams = states.shape[0]
    heads = states.shape[1]
    length = WINDOW_LENGTH
    rows = streams * length
    moved = move_states(states, dest_slot)
    features_all = lax.all_gather(tokens, "tp", axis=1, tiled=True)
    pieces = (
        lax.all_gather(qkv_weight, "stream", axis=0, tiled=True),
        lax.all_gather(gate_weight, "stream", axis=0, tiled=True),
    )
    count = pieces[1].shape[0]
    qkv_part = jnp.dot(
        features_all, pieces[0].reshape(count, -1), preferred_element_type=jnp.float32
    )
    gate_part = jnp.dot(features_all, pieces[1], preferred_element_type=jnp.float32)
    activated = jax.nn.silu(qkv_part).astype(jnp.bfloat16).reshape(streams, length, 3, heads, HD)
    positions = jnp.arange(length, dtype=jnp.int32)
    live = positions[None, :] < valid[:, None]
    live_half = live.astype(jnp.bfloat16)[:, :, None, None]
    live_full = live.astype(jnp.float32)
    query = activated[:, :, 0]
    lookup_vectors = activated[:, :, 1] * live_half
    values = activated[:, :, 2] * live_half
    decay = log_decay.reshape(heads, streams, length).transpose(1, 0, 2) * live_full[:, None, :]
    lower_ones = (positions[:, None] <= positions[None, :]).astype(jnp.float32)
    cumulative = jnp.einsum("shu,ut->sht", decay, lower_ones, precision=lax.Precision.HIGHEST)
    scores = jnp.einsum(
        "sthd,suhd->shtu", query, lookup_vectors, preferred_element_type=jnp.float32
    )
    causal = positions[:, None] >= positions[None, :]
    gap = cumulative[:, :, :, None] - cumulative[:, :, None, :]
    weights = jnp.where(causal, jnp.exp(jnp.minimum(gap, 0.0)), 0.0)
    probs = (scores * weights).astype(jnp.bfloat16)
    intra = jnp.einsum("shtu,suhd->sthd", probs, values, preferred_element_type=jnp.float32)
    query_full = query.astype(jnp.float32)
    carried = jnp.einsum("sthd,shde->sthe", query_full, moved, precision=lax.Precision.HIGHEST)
    carried = carried * jnp.exp(cumulative).transpose(0, 2, 1)[:, :, :, None]
    attended = intra + carried
    final_log = cumulative[:, :, length - 1 :]
    weighted_keys = (
        lookup_vectors.astype(jnp.float32)
        * jnp.exp(final_log - cumulative).transpose(0, 2, 1)[:, :, :, None]
    )
    updated = jnp.exp(final_log)[:, :, :, None] * moved + jnp.einsum(
        "sthd,sthe->shde",
        weighted_keys,
        values.astype(jnp.float32),
        precision=lax.Precision.HIGHEST,
    )
    mean_square = jnp.mean(attended * attended, axis=-1, keepdims=True)
    normed = attended * lax.rsqrt(mean_square + 1e-05)
    gates = jax.nn.sigmoid(gate_part).reshape(streams, length, heads, HD)
    hidden = (
        (normed * gates * live_full[:, :, None, None])
        .astype(jnp.bfloat16)
        .reshape(rows, heads * HD)
    )
    all_heads = lax.all_gather(hidden, "tp", axis=1, tiled=True)
    group_rows = lax.all_gather(out_weight, "stream", axis=1, tiled=True)
    full_rows = lax.all_to_all(group_rows, "tp", split_axis=1, concat_axis=0, tiled=True)
    mixed = jnp.dot(all_heads, full_rows, preferred_element_type=jnp.float32).astype(jnp.bfloat16)
    return (mixed, updated)


def solution(mesh):
    return jax.shard_map(
        body,
        mesh=mesh,
        in_specs=(
            P("stream", "tp"),
            P("stream", None, "tp"),
            P("stream", "tp"),
            P("tp", "stream"),
            P("tp", "stream"),
            P("stream", "tp", None, None),
            P("stream"),
            P("stream"),
        ),
        out_specs=(P("stream", "tp"), P("stream", "tp", None, None)),
        check_vma=False,
    )
```

profile of v0, /device:TPU:0, one launch (start us, length us, event | category | flops | bytes accessed | tf_op | source)
XLA Modules:
  0.0 544.0 jit_solution(4965468959096347591)
XLA Ops:
  7.2 0.0 all-gather.10.cloned.1.call-start
  7.2 0.7 all-gather.10.cloned.1.call-update
  7.9 0.0 all-gather.6.cloned.1.call-start
  8.0 0.7 all-gather.6.cloned.1.call-update
  8.7 0.0 all-gather.8.cloned.1.call-start
  8.7 1.4 copy.98
  10.2 0.2 convert_reduce_fusion
  10.4 0.6 scatter_custom_fusion
  11.0 0.7 all_to_all.23
  11.7 5.2 all-to-all-start
  16.8 2.6 broadcast_in_dim.13
  19.4 6.5 %scatter_fusion = f32[16,8,64,64]{3,2,1,0:T(8,128)} fusion(f32[16,8,64,64]{3,2,1,0:T(8,128)} %broadcast_in_dim.13, s32[12]{0:T(128)S(1)} %compare_select_fusion.1, f32[12,8,64,64]{3,2,1,0:T(8,128)S(1)} %copy-done.3), kind=kCustom, calls=%fused_computation.1 | custom fusion | bytes 4718640 | tf_op jit(solution)/shard_map/scatter | solution.py:22
  25.9 7.2 %reshape.182 = f32[8,1,65536]{2,1,0:T(1,128)} reshape(f32[8,2,8,64,64]{4,3,2,1,0:T(8,128)} %bitcast.69) | data formatting | bytes 4194304
  33.1 4.2 all-to-all-start.1
  37.3 0.0 all-gather.14.cloned.1.call-start
  37.4 0.9 copy.108
  38.3 0.0 all-gather.12.cloned.1.call-start
  38.4 0.7 fusion.27
  39.1 0.2 fusion.22
  39.2 0.1 slice.23
  39.3 0.2 copy.124
  39.5 0.2 copy-done.7
  39.7 0.1 exponential_bitcast_fusion.1
  39.7 0.6 copy.113
  40.4 0.6 iota_compare_fusion.1
  41.0 0.5 broadcast.114
  41.5 0.7 reduce.3
  42.2 0.1 reshape.138
  42.2 0.5 fusion.29
  42.8 24.0 %all-to-all-done.1 = f32[8,1,65536]{2,1,0:T(1,128)S(1)} async-done(((f32[8,1,65536]{2,1,0:T(1,128)}), f32[8,1,65536]{2,1,0:T(1,128)S(1)}, u32[]{:S(2)}, u32[]{:S(2)}) %all-to-all-start.1) | async-done | bytes 2097184 | tf_op jit(solution)/shard_map/all_to_all | solution.py:28
  66.7 1.3 copy-done.1
  68.0 0.5 broadcast.115
  68.5 7.1 %reduce.4 = f32[8,65536]{1,0:T(8,128)S(1)} reduce(f32[8,1,65536]{2,1,0:T(1,128)} %copy-done.1, f32[]{:T(128)} %broadcast.115), dimensions={1}, to_apply=%all_to_all.25.reduce_sub_computation | reduce | bytes 4194308 | tf_op jit(solution)/shard_map/all_to_all | solution.py:28
  75.6 3.7 reshape.183
  79.4 0.4 broadcast_in_dim.11
  79.8 4.8 scatter_fusion.1
  84.6 0.0 all-gather.10.cloned.1.call-done
  84.6 137.1 %all-gather.6.cloned.1.call-done = bf16[1536,3072]{1,0:T(8,128)(2,1)} async-done(((bf16[1536,768]{1,0:T(8,128)(2,1)}), bf16[1536,3072]{1,0:T(8,128)(2,1)}) %all-gather.6.cloned.1.call-update) | async-done | bytes 9437200 | tf_op jit(solution)/shard_map/all_gather | solution.py:43
  221.7 10.8 %fusion.2 = f32[1536,512]{1,0:T(8,128)} fusion(bf16[1536,3072]{1,0:T(8,128)(2,1)} %all-gather.6.cloned.1.call-done, bf16[3072,512]{1,0:T(8,128)(2,1)} %all-gather.10.cloned.1.call-done), kind=kOutput, calls=%fused_computation.10 | convolution fusion | flops 4834197504 | bytes 15728640 | tf_op jit(solution)/shard_map/dot_general | solution.py:52
  232.5 5.7 %reshape.170 = f32[12,128,8,64]{3,2,1,0:T(8,128)} reshape(f32[1536,512]{1,0:T(8,128)} %fusion.2) | data formatting | bytes 6291456 | tf_op jit(solution)/shard_map/reshape | solution.py:89
  238.1 6.1 %copy.106 = f32[12,128,8,64]{1,3,2,0:T(8,128)} copy(f32[12,128,8,64]{3,2,1,0:T(8,128)} %reshape.170) | data formatting | bytes 6291456 | tf_op jit(solution)/shard_map/reshape | solution.py:89
  244.2 38.1 %all-gather.8.cloned.1.call-done = bf16[3072,3,512]{0,2,1:T(8,128)(2,1)} async-done(((bf16[384,3,512]{0,2,1:T(8,128)(2,1)}), bf16[3072,3,512]{0,2,1:T(8,128)(2,1)}) %all-gather.8.cloned.1.call-update) | async-done | bytes 9437200 | tf_op jit(solution)/shard_map/all_gather | solution.py:45
  282.4 22.6 %multiply_convert_fusion = bf16[1536,1536]{1,0:T(8,128)(2,1)} fusion(bf16[1536,3072]{1,0:T(8,128)(2,1)} %all-gather.6.cloned.1.call-done, bf16[3072,1536]{0,1:T(8,128)(2,1)} %bitcast.76), kind=kOutput, calls=%fused_computation.3 | convolution fusion | flops 14507311104 | bytes 23592960 | tf_op jit(solution)/shard_map/dot_general | solution.py:49
  304.9 6.7 %copy.99 = bf16[1536,1536]{0,1:T(8,128)(2,1)} copy(bf16[1536,1536]{1,0:T(8,128)(2,1)} %multiply_convert_fusion) | data formatting | bytes 9437184 | tf_op jit(solution)/shard_map/convert_element_type | solution.py:53
  311.7 9.5 %reshape.136 = bf16[12,128,3,8,64]{1,0,4,3,2:T(8,128)(2,1)} reshape(bf16[1536,1536]{0,1:T(8,128)(2,1)} %copy.99) | data formatting | bytes 9437184 | tf_op jit(solution)/shard_map/reshape | solution.py:53
  321.2 3.3 slice.21
  324.4 3.1 fusion.14
  327.6 4.9 convert_multiply_fusion
  332.4 9.0 %fusion.3 = f32[12,8,64,128]{3,2,1,0:T(8,128)} fusion(f32[12,8,128]{2,1,0:T(8,128)S(1)} %fusion.22, pred[128,128]{1,0:T(8,128)(4,1)} %iota_compare_fusion.1, bf16[12,128,8,64]{1,0,3,2:T(8,128)(2,1)} %get-tuple-element.15, bf16[12,128,1,8,64]{1,0,4,3,2:T(8,128)(2,1)} %slice.21, bf16[12,128,8,64]{1,0,3,2:T(8,128)(2,1)} %fusion.14), kind=kOutput, calls=%fused_computation.11 | convolution fusion | flops 410517504 | bytes 7929856 | tf_op jit(solution)/shard_map/shtu,suhd->sthd/dot_general | solution.py:71
  341.4 5.3 multiply_reduce_fusion
  346.8 0.8 multiply_convert_fusion.3
  347.6 1.1 copy.107
  348.7 1.6 copy.144
  350.3 4.8 all-to-all-start.2
  355.2 0.1 copy.123
  355.3 0.1 copy.111
  355.4 1.9 slice.24
  357.3 2.8 copy.122
  360.1 146.4 %all-to-all-done.2 = bf16[512,4,768]{0,2,1:T(8,128)(2,1)} async-done(((bf16[512,4,768]{0,2,1:T(8,128)(2,1)}), bf16[512,4,768]{0,2,1:T(8,128)(2,1)}, u32[]{:S(2)}, u32[]{:S(2)}) %all-to-all-start.2) | async-done | bytes 3145760 | tf_op jit(solution)/shard_map/all_to_all | solution.py:97
  506.5 4.6 copy.109
  511.1 8.4 %multiply_add_fusion = f32[12,8,64,64]{2,3,1,0:T(8,128)} fusion(f32[12,8,64,64]{2,3,1,0:T(8,128)S(1)} %copy.122, f32[12,128,8,64]{1,0,3,2:T(8,128)} %get-tuple-element.14, f32[12,8]{1,0:T(8,128)S(1)} %copy.111, bf16[12,128,8,64]{1,0,3,2:T(8,128)(2,1)} %fusion.14), kind=kOutput, calls=%fused_computation.16 | convolution fusion | flops 604766208 | bytes 7864704 | tf_op jit(solution)/shard_map/sthd,sthe->shde/dot_general | solution.py:81
  519.6 3.7 copy.117
  523.3 4.8 all-gather.12.cloned.1.call-done
  528.0 9.2 %convolution_convert_fusion = bf16[1536,768]{1,0:T(8,128)(2,1)} fusion(bf16[1536,2048]{0,1:T(8,128)(2,1)} %all-gather.12.cloned.1.call-done, bf16[2048,768]{1,0:T(8,128)(2,1)S(1)} %bitcast.74), kind=kOutput, calls=%fused_computation.6 | convolution fusion | flops 4833017856 | bytes 11796480 | tf_op jit(solution)/shard_map/dot_general | solution.py:98
  (33 shorter events, 0.2 us)
Async XLA Ops:
  7.2 1.6 copy-start.4
  7.2 3.0 copy-start.12
  7.2 77.4 %all-gather.10.cloned.1.call-start = ((), (), s32[]{:S(2)}) async-start(), calls=%async_computation.5 | async-start | bytes 3538944 | tf_op jit(solution)/shard_map/all_gather | solution.py:46
  7.9 213.8 %all-gather.6.cloned.1.call-start = ((), (), s32[]{:S(2)}) async-start(), calls=%async_computation.3 | async-start | bytes 11796480 | tf_op jit(solution)/shard_map/all_gather | solution.py:43
  8.7 273.7 %all-gather.8.cloned.1.call-start = ((), (), s32[]{:S(2)}) async-start(), calls=%async_computation.4 | async-start | bytes 10616832 | tf_op jit(solution)/shard_map/all_gather | solution.py:45
  10.1 9.3 %copy-start.3 = (f32[12,8,64,64]{3,2,1,0:T(8,128)S(1)}, f32[12,8,64,64]{3,2,1,0:T(8,128)}, u32[]{:S(2)}) copy-start(f32[12,8,64,64]{3,2,1,0:T(8,128)} %param.13) | copy-start | bytes 4718596
  11.7 21.5 %all-to-all-start = ((s32[8,1,2]{2,1,0:T(1,128)}), s32[8,1,2]{2,1,0:T(1,128)S(1)}, u32[]{:S(2)}, u32[]{:S(2)}) async-start(s32[8,1,2]{2,1,0:T(1,128)} %bitcast.8), calls=%async_computation | async-start | bytes 8192 | tf_op jit(solution)/shard_map/all_to_all | solution.py:29
  33.1 4.2 copy-start.5
  33.1 5.3 copy-start.11
  33.1 5.9 %copy-start.9 = (f32[8,1536]{1,0:T(8,128)S(1)}, f32[8,1536]{1,0:T(8,128)}, u32[]{:S(2)}) copy-start(f32[8,1536]{1,0:T(8,128)} %param.12) | copy-start | bytes 147460
  33.1 33.6 %all-to-all-start.1 = ((f32[8,1,65536]{2,1,0:T(1,128)}), f32[8,1,65536]{2,1,0:T(1,128)S(1)}, u32[]{:S(2)}, u32[]{:S(2)}) async-start(f32[8,1,65536]{2,1,0:T(1,128)} %reshape.182), calls=%async_computation.1 | async-start | bytes 4194304 | tf_op jit(solution)/shard_map/all_to_all | solution.py:28
  37.3 313.0 %all-gather.14.cloned.1.call-start = ((), (), s32[]{:S(2)}) async-start(), calls=%async_computation.7 | async-start | bytes 3538944 | tf_op jit(solution)/shard_map/all_gather | solution.py:96
  38.3 489.7 %all-gather.12.cloned.1.call-start = ((), (), s32[]{:S(2)}) async-start(), calls=%async_computation.6 | async-start | bytes 7864320 | tf_op jit(solution)/shard_map/all_gather | solution.py:95
  39.1 0.6 copy-start.7
  66.7 1.3 copy-start.1
  321.2 3.3 copy-start.10
  324.4 3.1 copy-start.6
  341.4 5.4 copy-start
  341.4 5.4 copy-start.8
  350.3 156.2 %all-to-all-start.2 = ((bf16[512,4,768]{0,2,1:T(8,128)(2,1)}), bf16[512,4,768]{0,2,1:T(8,128)(2,1)}, u32[]{:S(2)}, u32[]{:S(2)}) async-start(bf16[512,4,768]{0,2,1:T(8,128)(2,1)} %bitcast.73), calls=%async_computation.2 | async-start | bytes 6291456 | tf_op jit(solution)/shard_map/all_to_all | solution.py:97
  519.6 8.5 %copy-start.2 = (bf16[4,512,768]{2,1,0:T(8,128)(2,1)S(1)}, bf16[4,512,768]{2,1,0:T(8,128)(2,1)}, u32[]{:S(2)}) copy-start(bf16[4,512,768]{2,1,0:T(8,128)(2,1)} %copy.109) | copy-start | bytes 9437188
Sparse Core Ops, SparseCore 0:
  9.9 37.7 all-gather.9
  49.3 172.3 all-gather.5
  223.6 58.7 all-gather.7
  284.1 32.3 all-gather.13
  350.4 177.5 all-gather.11
where the time goes:
time: 552 us; the launch traced here: 544 us
  waiting for transfers between devices  352 us (64%)
  local copies, waits for them, and re-layouts  79.4 us (14%)
  matrix products  65.5 us (12%)
  other arithmetic  18.7 us (3%)
  starting transfers between devices  14.4 us (3%)
  between operations  14.2 us (3%)
    all_to_all x1, waiting for transfers between devices, body(): lax.all_to_all(group_rows, 'tp', split_axis=1, concat_axis=0, tiled=True)  146 us
    all_gather x1, waiting for transfers between devices, body(): features_all = lax.all_gather(tokens, 'tp', axis=1, tiled=True)  137 us
    all_gather x1, waiting for transfers between devices, body(): lax.all_gather(qkv_weight, 'stream', axis=0, tiled=True)  38.1 us
    unnamed x35, local copies, waits for them, and re-layouts  24.8 us
    all_to_all x1, waiting for transfers between devices, move_states(): lax.all_to_all(outgoing, 'stream', split_axis=0, concat_axis=0, tiled=True)  24 us
    dot_general x1, matrix products, body(): jnp.dot(features_all, pieces[0].reshape(count, -1), preferred_element_typ...  22.6 us
    reshape x2, local copies, waits for them, and re-layouts, body(): gates = jax.nn.sigmoid(gate_part).reshape(streams, length, heads, HD)  11.8 us
  transfers between devices with their start and end apart: 8, of which 5 were waited for; matrix products, arithmetic and copies ran while one was open for 28% of the time, Pallas kernels for 0%

commit v1 on v0

--- a/solution.py
+++ b/solution.py
@@ -1,3 +1,4 @@
+import functools
 import jax
 import jax.numpy as jnp
 from jax import lax
@@ -5,6 +6,26 @@
 
 HD = 64
 WINDOW_LENGTH = 128
+
+
+def enter_shards_here(inp, mesh_name):
+    world_n = lax.axis_size(mesh_name)
+    trail = [inp]
+    for d in range(world_n - 1):
+        trail.append(
+            lax.ppermute(
+                trail[-1],
+                axis_name=mesh_name,
+                perm=[(dev, (dev + 1) % world_n) for dev in range(world_n)],
+            )
+        )
+    near = jnp.roll(
+        jnp.concatenate(trail[::-1], 1), (lax.axis_index(mesh_name) + 1) * inp.shape[1], 1
+    )
+    return near
+
+
+shape_packet = functools.partial(enter_shards_here, mesh_name="tp")
 
 
 def move_states(states, dest_slot):
@@ -40,7 +61,7 @@
     length = WINDOW_LENGTH
     rows = streams * length
     moved = move_states(states, dest_slot)
-    features_all = lax.all_gather(tokens, "tp", axis=1, tiled=True)
+    features_all = shape_packet(tokens)
     pieces = (
         lax.all_gather(qkv_weight, "stream", axis=0, tiled=True),
         lax.all_gather(gate_weight, "stream", axis=0, tiled=True),

time: 552 us -> 507 us (0.918)
  waiting for transfers between devices: 352 us -> 281 us
  local copies, waits for them, and re-layouts: 79.4 us -> 102 us
    all_gather x1 -> x0, waiting for transfers between devices: 137 us -> none  [body(): features_all = lax.all_gather(tokens, 'tp', axis=1, tiled=True)]
    ppermute x0 -> x3, waiting for transfers between devices: none -> 108 us  [enter_shards_here(): lax.ppermute(trail[-1], axis_name=mesh_name, perm=[(dev, (dev + 1) % worl...]
    all_gather x1, waiting for transfers between devices: 38.1 us -> 0.01 us  [body(): lax.all_gather(qkv_weight, 'stream', axis=0, tiled=True)]
    unnamed x35 -> x48, local copies, waits for them, and re-layouts: 24.8 us -> 46.3 us
  transfers between devices with their start and end apart: 8 -> 10, of which waited for: 5 -> 5; matrix products, arithmetic and copies ran while one was open for 28% -> 34% of each run, Pallas kernels for 0% -> 0%
where the time goes in v1:
time: 507 us; the launch traced here: 497 us
  waiting for transfers between devices  281 us (55%)
  local copies, waits for them, and re-layouts  102 us (20%)
  matrix products  64 us (13%)
  other arithmetic  18.8 us (4%)
  starting transfers between devices  16.3 us (3%)
  between operations  14.2 us (3%)
    all_to_all x1, waiting for transfers between devices, body(): lax.all_to_all(group_rows, 'tp', split_axis=1, concat_axis=0, tiled=True)  143 us
    ppermute x3, waiting for transfers between devices, enter_shards_here(): lax.ppermute(trail[-1], axis_name=mesh_name, perm=[(dev, (dev + 1) % worl...  108 us
    unnamed x48, local copies, waits for them, and re-layouts  46.3 us
    all_to_all x1, waiting for transfers between devices, move_states(): lax.all_to_all(outgoing, 'stream', split_axis=0, concat_axis=0, tiled=True)  25.5 us
    dot_general x1, matrix products, body(): jnp.dot(features_all, pieces[0].reshape(count, -1), preferred_element_typ...  21.9 us
    reshape x2, local copies, waits for them, and re-layouts, body(): gates = jax.nn.sigmoid(gate_part).reshape(streams, length, heads, HD)  11.7 us
    dot_general x1, matrix products, body(): jnp.dot(features_all, pieces[1], preferred_element_type=jnp.float32)  10.3 us
  transfers between devices with their start and end apart: 10, of which 5 were waited for; matrix products, arithmetic and copies ran while one was open for 34% of the time, Pallas kernels for 0%

profile of v1, /device:TPU:0, one launch (start us, length us, event | category | flops | bytes accessed | tf_op | source)
XLA Modules:
  0.0 496.9 jit_solution(10862066982848961274)
XLA Ops:
  7.2 0.7 all-gather.7.cloned.1.call-update
  8.0 2.4 copy.98
  10.4 3.1 collective-permute-start
  13.5 53.3 %collective-permute-done = bf16[1536,768]{1,0:T(8,128)(2,1)S(1)} collective-permute-done((bf16[1536,768]{1,0:T(8,128)(2,1)S(1)}, bf16[1536,768]{1,0:T(8,128)(2,1)S(1)}, u32[]{:S(2)}, u32[]{:S(2)}) %collective-permute-start) | collective-permute-done | bytes 2359328 | tf_op jit(solution)/shard_map/ppermute | solution.py:16
  66.7 1.4 copy-done.3
  68.1 54.3 %collective-permute-done.1 = bf16[1536,768]{1,0:T(8,128)(2,1)} collective-permute-done((bf16[1536,768]{1,0:T(8,128)(2,1)S(1)}, bf16[1536,768]{1,0:T(8,128)(2,1)}, u32[]{:S(2)}, u32[]{:S(2)}) %collective-permute-start.1) | collective-permute-done | bytes 2359328 | tf_op jit(solution)/shard_map/ppermute | solution.py:16
  122.5 0.2 convert_reduce_fusion
  122.7 0.6 scatter_custom_fusion
  123.3 0.7 all_to_all.23
  124.0 3.5 all-to-all-start
  127.5 2.5 broadcast_in_dim.13
  129.9 6.3 %scatter_fusion = f32[16,8,64,64]{3,2,1,0:T(8,128)} fusion(f32[16,8,64,64]{3,2,1,0:T(8,128)} %broadcast_in_dim.13, s32[12]{0:T(128)S(1)} %compare_select_fusion.1, f32[12,8,64,64]{3,2,1,0:T(8,128)S(1)} %copy-done.7), kind=kCustom, calls=%fused_computation.1 | custom fusion | bytes 4718640 | tf_op jit(solution)/shard_map/scatter | solution.py:43
  136.2 7.2 %reshape.182 = f32[8,1,65536]{2,1,0:T(1,128)} reshape(f32[8,2,8,64,64]{4,3,2,1,0:T(8,128)} %bitcast.64) | data formatting | bytes 4194304
  143.4 4.3 all-to-all-start.1
  147.8 0.9 copy.108
  148.9 0.7 fusion.38
  149.5 0.2 fusion.33
  149.8 0.2 copy.124
  149.9 0.2 copy-done.10
  150.2 0.6 copy.113
  150.8 0.6 iota_compare_fusion.1
  151.5 0.5 broadcast.118
  152.0 0.6 reduce.3
  152.6 0.5 fusion.40
  153.1 25.5 %all-to-all-done.1 = f32[8,1,65536]{2,1,0:T(1,128)S(1)} async-done(((f32[8,1,65536]{2,1,0:T(1,128)}), f32[8,1,65536]{2,1,0:T(1,128)S(1)}, u32[]{:S(2)}, u32[]{:S(2)}) %all-to-all-start.1) | async-done | bytes 2097184 | tf_op jit(solution)/shard_map/all_to_all | solution.py:49
  178.6 1.3 copy-done.5
  179.9 0.5 broadcast.119
  180.4 7.3 %reduce.4 = f32[8,65536]{1,0:T(8,128)S(1)} reduce(f32[8,1,65536]{2,1,0:T(1,128)} %copy-done.5, f32[]{:T(128)} %broadcast.119), dimensions={1}, to_apply=%all_to_all.25.reduce_sub_computation | reduce | bytes 4194308 | tf_op jit(solution)/shard_map/all_to_all | solution.py:49
  187.7 3.6 reshape.183
  191.3 0.4 broadcast_in_dim.11
  191.7 5.1 %scatter_fusion.1 = f32[13,8,64,64]{3,2,1,0:T(8,128)S(1)} fusion(f32[13,8,64,64]{3,2,1,0:T(8,128)S(1)} %broadcast_in_dim.11, s32[16]{0:T(128)} %fusion.40, f32[16,8,64,64]{3,2,1,0:T(8,128)} %bitcast.65), kind=kCustom, calls=%fused_computation.2 | custom fusion | bytes 6291520 | tf_op jit(solution)/shard_map/scatter | solution.py:54
  196.8 3.4 constant_dynamic-update-slice_fusion.7
  200.2 3.5 constant_dynamic-update-slice_fusion.6
  203.7 1.6 constant_dynamic-update-slice_fusion.5
  205.3 0.9 copy-done.2
  206.2 1.6 constant_dynamic-update-slice_fusion.4
  207.8 3.3 constant_dynamic-update-slice_fusion.3
  211.1 3.2 constant_dynamic-update-slice_fusion.2
  214.3 1.7 constant_dynamic-update-slice_fusion.1
  216.1 1.6 constant_dynamic-update-slice_fusion
  217.6 10.3 %add_divide_fusion = f32[1536,512]{1,0:T(8,128)} fusion(bf16[3072,512]{1,0:T(8,128)(2,1)} %all-gather.7.cloned.1.call-done, bf16[1536,6144]{1,0:T(8,128)(2,1)} %constant_dynamic-update-slice_fusion, s32[]{:T(128)S(6)} %select_n.43), kind=kOutput, calls=%fused_computation.20 | convolution fusion | flops 4834197504 | bytes 15728644 | tf_op jit(solution)/shard_map/dot_general | solution.py:73
  227.9 5.6 %reshape.170 = f32[12,128,8,64]{3,2,1,0:T(8,128)} reshape(f32[1536,512]{1,0:T(8,128)} %add_divide_fusion) | data formatting | bytes 6291456 | tf_op jit(solution)/shard_map/reshape | solution.py:110
  233.5 6.1 %copy.106 = f32[12,128,8,64]{1,3,2,0:T(8,128)} copy(f32[12,128,8,64]{3,2,1,0:T(8,128)} %reshape.170) | data formatting | bytes 6291456 | tf_op jit(solution)/shard_map/reshape | solution.py:110
  239.6 21.9 %multiply_convert_fusion = bf16[1536,1536]{1,0:T(8,128)(2,1)} fusion(bf16[3072,1536]{0,1:T(8,128)(2,1)} %bitcast.71, bf16[1536,6144]{1,0:T(8,128)(2,1)} %constant_dynamic-update-slice_fusion, s32[]{:T(128)S(6)} %select_n.43), kind=kOutput, calls=%fused_computation.3 | convolution fusion | flops 14507311104 | bytes 23592964 | tf_op jit(solution)/shard_map/dot_general | solution.py:70
  261.6 6.7 %copy.99 = bf16[1536,1536]{0,1:T(8,128)(2,1)} copy(bf16[1536,1536]{1,0:T(8,128)(2,1)} %multiply_convert_fusion) | data formatting | bytes 9437184 | tf_op jit(solution)/shard_map/convert_element_type | solution.py:74
  268.2 9.4 %reshape.136 = bf16[12,128,3,8,64]{1,0,4,3,2:T(8,128)(2,1)} reshape(bf16[1536,1536]{0,1:T(8,128)(2,1)} %copy.99) | data formatting | bytes 9437184 | tf_op jit(solution)/shard_map/reshape | solution.py:74
  277.7 3.3 slice.21
  280.9 3.1 fusion.25
  284.0 4.9 convert_multiply_fusion
  288.9 8.7 %fusion.12 = f32[12,8,64,128]{3,2,1,0:T(8,128)} fusion(f32[12,8,128]{2,1,0:T(8,128)S(1)} %fusion.33, pred[128,128]{1,0:T(8,128)(4,1)} %iota_compare_fusion.1, bf16[12,128,8,64]{1,0,3,2:T(8,128)(2,1)} %get-tuple-element.15, bf16[12,128,1,8,64]{1,0,4,3,2:T(8,128)(2,1)} %slice.21, bf16[12,128,8,64]{1,0,3,2:T(8,128)(2,1)} %fusion.25), kind=kOutput, calls=%fused_computation.13 | convolution fusion | flops 410517504 | bytes 7929856 | tf_op jit(solution)/shard_map/shtu,suhd->sthd/dot_general | solution.py:92
  297.6 5.3 %multiply_reduce_fusion = (f32[12,128,8]{1,2,0:T(8,128)S(1)}, f32[12,128,8,64]{1,3,2,0:T(8,128)S(1)}) fusion(f32[12,128,8]{1,2,0:T(8,128)S(1)} %get-tuple-element.16, f32[13,8,64,64]{3,2,1,0:T(8,128)S(1)} %scatter_fusion.1, bf16[12,128,1,8,64]{1,0,4,3,2:T(8,128)(2,1)} %slice.21, f32[12,8,64,128]{3,2,1,0:T(8,128)} %fusion.12), kind=kOutput, calls=%fused_computation.21 | convolution fusion | flops 607113216 | bytes 9666560 | tf_op jit(solution)/shard_map/sthd,shde->sthe/dot_general | solution.py:94
  303.0 0.8 multiply_convert_fusion.3
  303.9 1.1 copy.107
  305.0 1.6 copy.144
  306.6 5.3 %all-to-all-start.2 = ((bf16[512,4,768]{0,2,1:T(8,128)(2,1)}), bf16[512,4,768]{0,2,1:T(8,128)(2,1)}, u32[]{:S(2)}, u32[]{:S(2)}) async-start(bf16[512,4,768]{0,2,1:T(8,128)(2,1)} %bitcast.68), calls=%async_computation.2 | async-start | bytes 6291456 | tf_op jit(solution)/shard_map/all_to_all | solution.py:118
  311.9 0.1 copy.123
  312.1 1.9 slice.24
  314.0 2.7 copy.122
  316.7 142.9 %all-to-all-done.2 = bf16[512,4,768]{0,2,1:T(8,128)(2,1)} async-done(((bf16[512,4,768]{0,2,1:T(8,128)(2,1)}), bf16[512,4,768]{0,2,1:T(8,128)(2,1)}, u32[]{:S(2)}, u32[]{:S(2)}) %all-to-all-start.2) | async-done | bytes 3145760 | tf_op jit(solution)/shard_map/all_to_all | solution.py:118
  459.6 4.7 copy.109
  464.3 8.4 %multiply_add_fusion = f32[12,8,64,64]{2,3,1,0:T(8,128)} fusion(f32[12,8,64,64]{2,3,1,0:T(8,128)S(1)} %copy.122, f32[12,128,8,64]{1,0,3,2:T(8,128)} %get-tuple-element.14, f32[12,8]{1,0:T(8,128)S(1)} %copy.111, bf16[12,128,8,64]{1,0,3,2:T(8,128)(2,1)} %fusion.25), kind=kOutput, calls=%fused_computation.18 | convolution fusion | flops 604766208 | bytes 7864704 | tf_op jit(solution)/shard_map/sthd,sthe->shde/dot_general | solution.py:102
  472.7 3.7 copy.117
  476.4 4.5 all-gather.9.cloned.1.call-done
  480.9 9.2 %convolution_convert_fusion = bf16[1536,768]{1,0:T(8,128)(2,1)} fusion(bf16[1536,2048]{0,1:T(8,128)(2,1)} %all-gather.9.cloned.1.call-done, bf16[2048,768]{1,0:T(8,128)(2,1)S(1)} %bitcast.69), kind=kOutput, calls=%fused_computation.10 | convolution fusion | flops 4833017856 | bytes 11796480 | tf_op jit(solution)/shard_map/dot_general | solution.py:119
  (50 shorter events, 0.7 us)
Async XLA Ops:
  7.2 3.2 copy-start.1
  7.2 115.3 %copy-start.15 = (s32[12]{0:T(128)S(1)}, s32[12]{0:T(128)}, u32[]{:S(2)}) copy-start(s32[12]{0:T(128)} %param.14) | copy-start | bytes 148
  7.2 210.5 %all-gather.7.cloned.1.call-start = ((), (), s32[]{:S(2)}) async-start(), calls=%async_computation.4 | async-start | bytes 3538944 | tf_op jit(solution)/shard_map/all_gather | solution.py:67
  7.9 231.7 %all-gather.5.cloned.1.call-start = ((), (), s32[]{:S(2)}) async-start(), calls=%async_computation.3 | async-start | bytes 10616832 | tf_op jit(solution)/shard_map/all_gather | solution.py:66
  10.4 56.3 %collective-permute-start = (bf16[1536,768]{1,0:T(8,128)(2,1)S(1)}, bf16[1536,768]{1,0:T(8,128)(2,1)S(1)}, u32[]{:S(2)}, u32[]{:S(2)}) collective-permute-start(bf16[1536,768]{1,0:T(8,128)(2,1)S(1)} %copy-done.1), channel_id=1, source_target_pairs={{0,1},{1,2},{2,3},{3,0},{4,5},{5,6},{6,7},{7,4},{8,9},{9,10},{10,1... | collective-permute-start | bytes 7077896 | tf_op jit(solution)/shard_map/ppermute | solution.py:16
  66.7 1.4 copy-start.3
  68.1 61.8 %copy-start.7 = (f32[12,8,64,64]{3,2,1,0:T(8,128)S(1)}, f32[12,8,64,64]{3,2,1,0:T(8,128)}, u32[]{:S(2)}) copy-start(f32[12,8,64,64]{3,2,1,0:T(8,128)} %param.13) | copy-start | bytes 4718596
  68.1 54.3 %collective-permute-start.1 = (bf16[1536,768]{1,0:T(8,128)(2,1)S(1)}, bf16[1536,768]{1,0:T(8,128)(2,1)}, u32[]{:S(2)}, u32[]{:S(2)}) collective-permute-start(bf16[1536,768]{1,0:T(8,128)(2,1)S(1)} %collective-permute-done), channel_id=1, source_target_pairs={{0,1},{1,2},{2,3},{3,0},{4,5},{5,6},{6,7},{7,4},{8,9},{9,10},{10,1... | collective-permute-start | bytes 7077896 | tf_op jit(solution)/shard_map/ppermute | solution.py:16
  122.5 74.3 %collective-permute-start.2 = (bf16[1536,768]{1,0:T(8,128)(2,1)}, bf16[1536,768]{1,0:T(8,128)(2,1)}, u32[]{:S(2)}, u32[]{:S(2)}) collective-permute-start(bf16[1536,768]{1,0:T(8,128)(2,1)} %collective-permute-done.1), channel_id=1, source_target_pairs={{0,1},{1,2},{2,3},{3,0},{4,5},{5,6},{6,7},{7,4},{8,9},{9,10},{10,1... | collective-permute-start | bytes 7077896 | tf_op jit(solution)/shard_map/ppermute | solution.py:16
  124.0 19.4 %all-to-all-start = ((s32[8,1,2]{2,1,0:T(1,128)}), s32[8,1,2]{2,1,0:T(1,128)S(1)}, u32[]{:S(2)}, u32[]{:S(2)}) async-start(s32[8,1,2]{2,1,0:T(1,128)} %bitcast.8), calls=%async_computation | async-start | bytes 8192 | tf_op jit(solution)/shard_map/all_to_all | solution.py:50
  143.4 4.4 copy-start.8
  143.4 5.4 %copy-start.14 = (s32[12]{0:T(128)S(1)}, s32[12]{0:T(128)}, u32[]{:S(2)}) copy-start(s32[12]{0:T(128)} %param.15) | copy-start | bytes 148
  143.4 6.1 %copy-start.12 = (f32[8,1536]{1,0:T(8,128)S(1)}, f32[8,1536]{1,0:T(8,128)}, u32[]{:S(2)}) copy-start(f32[8,1536]{1,0:T(8,128)} %param.12) | copy-start | bytes 147460
  143.4 35.2 %all-to-all-start.1 = ((f32[8,1,65536]{2,1,0:T(1,128)}), f32[8,1,65536]{2,1,0:T(1,128)S(1)}, u32[]{:S(2)}, u32[]{:S(2)}) async-start(f32[8,1,65536]{2,1,0:T(1,128)} %reshape.182), calls=%async_computation.1 | async-start | bytes 4194304 | tf_op jit(solution)/shard_map/all_to_all | solution.py:49
  147.7 158.8 %all-gather.11.cloned.1.call-start = ((), (), s32[]{:S(2)}) async-start(), calls=%async_computation.6 | async-start | bytes 3538944 | tf_op jit(solution)/shard_map/all_gather | solution.py:117
  148.8 332.2 %all-gather.9.cloned.1.call-start = ((), (), s32[]{:S(2)}) async-start(), calls=%async_computation.5 | async-start | bytes 7864320 | tf_op jit(solution)/shard_map/all_gather | solution.py:116
  149.5 0.6 copy-start.10
  178.6 1.3 copy-start.5
  200.2 3.5 copy-start.4
  203.7 2.5 copy-start.2
  277.7 3.3 copy-start.13
  280.9 3.1 copy-start.9
  297.6 5.4 %copy-start = (f32[12,128,8,64]{1,3,2,0:T(8,128)S(1)}, f32[12,128,8,64]{1,3,2,0:T(8,128)}, u32[]{:S(2)}) copy-start(f32[12,128,8,64]{1,3,2,0:T(8,128)} %copy.106) | copy-start | bytes 9437188
  297.6 5.4 %copy-start.11 = (f32[12,128]{1,0:T(8,128)S(1)}, f32[12,128]{1,0:T(8,128)}, u32[]{:S(2)}) copy-start(f32[12,128]{1,0:T(8,128)} %copy-done.10) | copy-start | bytes 18436
  306.6 153.1 %all-to-all-start.2 = ((bf16[512,4,768]{0,2,1:T(8,128)(2,1)}), bf16[512,4,768]{0,2,1:T(8,128)(2,1)}, u32[]{:S(2)}, u32[]{:S(2)}) async-start(bf16[512,4,768]{0,2,1:T(8,128)(2,1)} %bitcast.68), calls=%async_computation.2 | async-start | bytes 6291456 | tf_op jit(solution)/shard_map/all_to_all | solution.py:118
  472.7 8.2 %copy-start.6 = (bf16[4,512,768]{2,1,0:T(8,128)(2,1)S(1)}, bf16[4,512,768]{2,1,0:T(8,128)(2,1)}, u32[]{:S(2)}) copy-start(bf16[4,512,768]{2,1,0:T(8,128)(2,1)} %copy.109) | copy-start | bytes 9437188
Sparse Core Ops, SparseCore 0:
  9.9 35.0 all-gather.6
  46.8 60.5 all-gather.4
  150.5 43.9 all-gather.10
  306.7 174.2 all-gather.8
